TPU v7x, 512 devices: a whole 4x8x8 slice. The times are simulated.
512 devices in a mesh: exp: 16 (over y, core), space: 32 (over z, x).
Axes of the slice: x: 4, y: 8, z: 8, core: 2. Of those that a mesh axis runs over, the one named last changes fastest.
Arguments:
- initial: float32 [16, 4, 64, 64, 128], P('exp', None, 'space'), may hold values from -6 to 6
- cotangent: float32 [16, 4, 64, 64, 128], P('exp', None, 'space'), may hold values from -6 to 6
- permeability: float32 [64, 64, 128], P('space'), may hold values from 0.25 to 1.25
- labels: int32 [64, 64, 128], P('space'), may hold values from 0 to 511
- comp_scale: float32 [4], replicated, may hold values from 0.3 to 1
- coupling_mask: int32 [4, 4], replicated, may hold values from 0 to 1
- coupling_rate: float32 [4, 4], replicated, may hold values from 0.05 to 0.5
- dose: float32 [16], P('exp'), may hold values from 50 to 200
- inject_voxel: int32 [16], P('exp'), may hold values from 0 to 524287
- arrival: int32 [16], P('exp'), may hold values from 0 to 4
Outputs:
- concentration: float32 [16, 4, 64, 64, 128], P('exp', None, 'space')
- sensitivity: float32 [16, 4, 64, 64, 128], P('exp', None, 'space')
- perm_gradient: float32 [512], replicated
All inputs are finite; a program needn't handle non-finite values.
Results may differ from a plain program's by a relative error of at most 0.0003.
Values sent between devices are 32-bit elements; how exact they have to be, the bound alone decides.
No kernel may reach another device: no remote copies, remote signals or barrier semaphores. Data moves between devices by JAX's collectives and lax.ppermute only.
A program may use at most 64 MiB of HBM per device.

v0:
```python
import math
import jax
import jax.numpy as jnp
from jax import lax
from jax.sharding import PartitionSpec as P

STEPS = 5
LABELS = 512
time_step = 0.1


def extended(block, sides, width):
    for axis, dim in sides:
        count = lax.axis_size(axis)
        forward = [(i, i + 1) for i in range(count - 1)]
        backward = [(target, source) for source, target in forward]
        low = lax.ppermute(
            lax.slice_in_dim(block, block.shape[dim] - width, None, axis=dim), axis, forward
        )
        high = lax.ppermute(lax.slice_in_dim(block, 0, width, axis=dim), axis, backward)
        block = jnp.concatenate([low, block, high], axis=dim)
    return block


def sides(padded):
    return [
        padded[..., 2:, 1:-1, 1:-1],
        padded[..., :-2, 1:-1, 1:-1],
        padded[..., 1:-1, 2:, 1:-1],
        padded[..., 1:-1, :-2, 1:-1],
        padded[..., 1:-1, 1:-1, 2:],
        padded[..., 1:-1, 1:-1, :-2],
    ]


def widen(field):
    return jnp.pad(field, ((0, 0), (0, 0), (1, 1), (1, 1)))


def coupling(coupling_mask, coupling_rate):
    size = coupling_rate.shape[0]
    off = (
        coupling_mask.astype(jnp.float32) * coupling_rate * (1.0 - jnp.eye(size, dtype=jnp.float32))
    )
    return off - jnp.diag(jnp.sum(off, axis=1))


def on_device(
    initial,
    cotangent,
    permeability,
    labels,
    comp_scale,
    coupling_mask,
    coupling_rate,
    dose,
    inject_voxel,
    arrival,
):
    rows, wide, deep = permeability.shape
    perm_pad = extended(permeability, (("space", 0),), 1)
    perm_pad = jnp.pad(perm_pad, ((0, 0), (1, 1), (1, 1)))
    faces = [0.5 * (permeability + near) for near in sides(perm_pad)]
    mixing = coupling(coupling_mask, coupling_rate)
    scale = comp_scale[:, None, None, None]

    def laplace(padded, center):
        total = jnp.zeros_like(center)
        for coef, near in zip(faces, sides(padded)):
            total = total + coef * (near - center)
        return total

    offset = lax.axis_index("space") * rows
    plane_x = offset + lax.broadcasted_iota(jnp.int32, (rows, wide, deep), 0)
    plane_y = lax.broadcasted_iota(jnp.int32, (rows, wide, deep), 1)
    plane_z = lax.broadcasted_iota(jnp.int32, (rows, wide, deep), 2)
    flat = (plane_x * wide + plane_y) * deep + plane_z
    spot = (flat == inject_voxel[0]).astype(jnp.float32)
    state = initial[0]
    stored = []
    for step in range(STEPS):
        padded = widen(extended(state, (("space", 1),), 1))
        stored.append(padded)
        flow = scale * laplace(padded, state)
        flow = flow + jnp.einsum("cd,dxyz->cxyz", mixing, state, precision=lax.Precision.HIGHEST)
        pulse = jnp.where(step >= arrival[0], dose[0], 0.0) * time_step * spot
        state = state + time_step * flow
        state = state.at[0].add(pulse)
    adjoint = cotangent[0]
    grad = jnp.zeros((rows, wide, deep), jnp.float32)
    for step in reversed(range(STEPS)):
        padded_u = stored[step]
        padded_l = widen(extended(adjoint, (("space", 1),), 1))
        center_u = padded_u[:, 1:-1, 1:-1, 1:-1]
        product = jnp.zeros_like(adjoint)
        for near_l, near_u in zip(sides(padded_l), sides(padded_u)):
            product = product + (near_l - adjoint) * (near_u - center_u)
        grad = grad + jnp.sum(scale * product, axis=0)
        flow = scale * laplace(padded_l, adjoint)
        flow = flow + jnp.einsum("dc,dxyz->cxyz", mixing, adjoint, precision=lax.Precision.HIGHEST)
        adjoint = adjoint + time_step * flow
    weighted = -0.5 * time_step * grad * permeability
    flat_labels = labels.reshape(-1)
    summed = lax.psum(weighted, "exp")
    binned = jax.ops.segment_sum(summed.reshape(-1), flat_labels, num_segments=LABELS)
    total = lax.psum(binned, "space")
    norm_factor = math.sqrt(
        rows * lax.axis_size("space") * wide * deep * lax.axis_size("exp") / LABELS
    )
    return (state[None], adjoint[None], total / norm_factor)


def solution(mesh):
    return jax.shard_map(
        on_device,
        mesh=mesh,
        in_specs=(
            P("exp", None, "space", None, None),
            P("exp", None, "space", None, None),
            P("space", None, None),
            P("space", None, None),
            P(),
            P(),
            P(),
            P("exp"),
            P("exp"),
            P("exp"),
        ),
        out_specs=(P("exp", None, "space", None, None), P("exp", None, "space", None, None), P()),
        check_vma=False,
    )
```

profile of v0, /device:TPU:8, one launch (start us, length us, event | category | flops | bytes accessed | tf_op | source)
XLA Modules:
  0.0 471.1 jit_solution(2731218075138146100)
XLA Ops:
  8.0 3.5 collective-permute-start.2
  11.6 1.4 collective-permute-start
  13.0 1.1 copy.36
  14.2 4.6 collective-permute-start.13
  18.8 1.3 collective-permute-start.12
  20.3 4.6 collective-permute-start.3
  27.0 1.3 collective-permute-start.1
  28.7 5.2 %collective-permute-done.1 = f32[4,1,64,128]{3,0,2,1:T(4,128)S(1)} collective-permute-done((f32[4,1,64,128]{3,0,2,1:T(4,128)S(1)}, f32[4,1,64,128]{3,0,2,1:T(4,128)S(1)}, u32[]{:S(2)}, u32[]{:S(2)}) %collective-permute-start.1) | collective-permute-done | bytes 131104 | tf_op jit(solution)/shard_map/ppermute | solution.py:20
  35.5 1.3 scatter-add.24
  36.9 5.0 %collective-permute-start.5 = (f32[4,1,64,128]{3,0,2,1:T(4,128)S(1)}, f32[4,1,64,128]{3,0,2,1:T(4,128)S(1)}, u32[]{:S(2)}, u32[]{:S(2)}) collective-permute-start(f32[4,1,64,128]{3,0,2,1:T(4,128)S(1)} %get-tuple-element.86), channel_id=1, source_target_pairs={{0,1},{1,2},{2,3},{3,4},{4,5},{5,6},{6,7},{7,8},{8,9},{9,10},{10,1... | collective-permute-start | bytes 393224 | tf_op jit(solution)/shard_map/ppermute | solution.py:17
  41.9 1.3 collective-permute-start.4
  43.9 1.1 fusion.10
  45.8 7.3 %collective-permute-start.15 = (f32[4,1,64,128]{3,0,2,1:T(4,128)}, f32[4,1,64,128]{3,0,2,1:T(4,128)}, u32[]{:S(2)}, u32[]{:S(2)}) collective-permute-start(f32[4,1,64,128]{3,0,2,1:T(4,128)} %get-tuple-element.76), channel_id=1, source_target_pairs={{0,1},{1,2},{2,3},{3,4},{4,5},{5,6},{6,7},{7,8},{8,9},{9,10},{10,1... | collective-permute-start | bytes 393224 | tf_op jit(solution)/shard_map/ppermute | solution.py:17
  53.1 1.3 collective-permute-start.14
  57.7 2.8 scatter-add.25
  60.5 1.0 fusion.76
  61.5 6.0 %collective-permute-start.7 = (f32[4,1,64,128]{3,0,2,1:T(4,128)S(1)}, f32[4,1,64,128]{3,0,2,1:T(4,128)S(1)}, u32[]{:S(2)}, u32[]{:S(2)}) collective-permute-start(f32[4,1,64,128]{3,0,2,1:T(4,128)S(1)} %get-tuple-element.84), channel_id=1, source_target_pairs={{0,1},{1,2},{2,3},{3,4},{4,5},{5,6},{6,7},{7,8},{8,9},{9,10},{10,1... | collective-permute-start | bytes 393224 | tf_op jit(solution)/shard_map/ppermute | solution.py:17
  67.6 1.3 collective-permute-start.6
  68.9 1.7 select_maximum_fusion.6
  70.6 2.6 fusion.8
  74.0 5.2 %collective-permute-start.17 = (f32[4,1,64,128]{3,0,2,1:T(4,128)}, f32[4,1,64,128]{3,0,2,1:T(4,128)}, u32[]{:S(2)}, u32[]{:S(2)}) collective-permute-start(f32[4,1,64,128]{3,0,2,1:T(4,128)} %get-tuple-element.74), channel_id=1, source_target_pairs={{0,1},{1,2},{2,3},{3,4},{4,5},{5,6},{6,7},{7,8},{8,9},{9,10},{10,1... | collective-permute-start | bytes 393224 | tf_op jit(solution)/shard_map/ppermute | solution.py:17
  79.2 1.5 collective-permute-start.16
  83.9 2.8 scatter-add.26
  86.7 1.0 fusion.75
  87.7 4.6 collective-permute-start.9
  92.3 1.3 collective-permute-start.8
  93.6 1.7 select_maximum_fusion.4
  95.4 2.3 fusion.6
  98.4 6.8 %collective-permute-start.19 = (f32[4,1,64,128]{3,0,2,1:T(4,128)}, f32[4,1,64,128]{3,0,2,1:T(4,128)}, u32[]{:S(2)}, u32[]{:S(2)}) collective-permute-start(f32[4,1,64,128]{3,0,2,1:T(4,128)} %get-tuple-element.72), channel_id=1, source_target_pairs={{0,1},{1,2},{2,3},{3,4},{4,5},{5,6},{6,7},{7,8},{8,9},{9,10},{10,1... | collective-permute-start | bytes 393224 | tf_op jit(solution)/shard_map/ppermute | solution.py:17
  105.2 1.4 collective-permute-start.18
  106.7 2.5 multiply_reduce_fusion.2
  112.3 2.8 scatter-add.29
  115.2 1.0 fusion.74
  116.2 6.0 %collective-permute-start.11 = (f32[4,1,64,128]{3,0,2,1:T(4,128)S(1)}, f32[4,1,64,128]{3,0,2,1:T(4,128)S(1)}, u32[]{:S(2)}, u32[]{:S(2)}) collective-permute-start(f32[4,1,64,128]{3,0,2,1:T(4,128)S(1)} %get-tuple-element.80), channel_id=1, source_target_pairs={{0,1},{1,2},{2,3},{3,4},{4,5},{5,6},{6,7},{7,8},{8,9},{9,10},{10,1... | collective-permute-start | bytes 393224 | tf_op jit(solution)/shard_map/ppermute | solution.py:17
  122.3 1.3 collective-permute-start.10
  123.6 1.7 select_maximum_fusion.2
  125.4 2.3 fusion.4
  127.7 6.7 %collective-permute-start.21 = (f32[4,1,64,128]{3,0,2,1:T(4,128)S(1)}, f32[4,1,64,128]{3,0,2,1:T(4,128)S(1)}, u32[]{:S(2)}, u32[]{:S(2)}) collective-permute-start(f32[4,1,64,128]{3,0,2,1:T(4,128)S(1)} %get-tuple-element.70), channel_id=1, source_target_pairs={{0,1},{1,2},{2,3},{3,4},{4,5},{5,6},{6,7},{7,8},{8,9},{9,10},{10,1... | collective-permute-start | bytes 393224 | tf_op jit(solution)/shard_map/ppermute | solution.py:17
  134.4 1.6 collective-permute-start.20
  136.1 1.9 multiply_reduce_fusion.3
  138.0 1.9 multiply_reduce_fusion.1
  142.1 1.4 collective-permute-done.20
  145.9 2.2 fusion.12
  148.2 1.1 fusion.2
  149.5 1.3 scatter-add.36
  152.3 122.5 %all-reduce.13.cloned.1.call-done = f32[16384]{0:T(1024)} async-done(((f32[16384]{0:T(1024)}), f32[16384]{0:T(1024)}) %all-reduce.13.cloned.1.call-update) | async-done | bytes 65552 | tf_op jit(solution)/shard_map/psum | solution.py:104
  274.8 113.6 %scatter_custom_fusion = f32[512]{0:T(512)S(1)} fusion(s32[16384]{0:T(1024)} %bitcast.74, f32[16384]{0:T(1024)} %all-reduce.13.cloned.1.call-done, f32[]{:T(128)} %constant.150.clone.1), kind=kCustom, calls=%fused_computation.191 | custom fusion | flops 16384 | bytes 2560 | tf_op jit(solution)/shard_map/scatter-add | solution.py:105
  388.3 75.4 %psum.15 = f32[512]{0:T(512)S(1)} all-reduce(f32[512]{0:T(512)S(1)} %scatter_custom_fusion), channel_id=1, replica_groups=mesh['exp'=16,'space'=32] {'space'}, use_global_device_ids=true, to_apply=%region_8.9 | all-reduce | flops 512 | bytes 4096 | tf_op jit(solution)/shard_map/psum | solution.py:106
  (252 shorter events, 22.0 us)
Async XLA Ops:
  7.2 12.9 %copy-start.57 = (f32[1,4,2,64,128]{4,3,2,1,0:T(8,128)S(1)}, f32[1,4,2,64,128]{4,3,2,1,0:T(8,128)}, u32[]{:S(2)}) copy-start(f32[1,4,2,64,128]{4,3,2,1,0:T(8,128)} %param.20) | copy-start | bytes 786436
  7.2 267.6 %all-reduce.13.cloned.1.call-start = ((), (), s32[]{:S(2)}) async-start(), calls=%async_computation | async-start | bytes 131072 | tf_op jit(solution)/shard_map/psum | solution.py:104
  8.0 16.8 %copy-start.95 = (f32[4,4]{1,0:T(4,128)S(1)}, f32[4,4]{1,0:T(4,128)}, u32[]{:S(2)}) copy-start(f32[4,4]{1,0:T(4,128)} %param.26) | copy-start | bytes 196
  8.0 16.8 %copy-start.96 = (s32[4,4]{1,0:T(4,128)S(1)}, s32[4,4]{1,0:T(4,128)}, u32[]{:S(2)}) copy-start(s32[4,4]{1,0:T(4,128)} %param.25) | copy-start | bytes 196
  8.0 19.0 %collective-permute-start.2 = (f32[1,64,128]{2,1,0:T(8,128)S(1)}, f32[1,64,128]{2,1,0:T(8,128)S(1)}, u32[]{:S(2)}, u32[]{:S(2)}) collective-permute-start(f32[1,64,128]{2,1,0:T(8,128)S(1)} %get-tuple-element.92), channel_id=1, source_target_pairs={{0,1},{1,2},{2,3},{3,4},{4,5},{5,6},{6,7},{7,8},{8,9},{9,10},{10,1... | collective-permute-start | bytes 98312 | tf_op jit(solution)/shard_map/ppermute | solution.py:17
  11.6 16.8 %copy-start.28 = (f32[2,64,128]{2,1,0:T(8,128)S(1)}, f32[2,64,128]{2,1,0:T(8,128)}, u32[]{:S(2)}) copy-start(f32[2,64,128]{2,1,0:T(8,128)} %param.22) | copy-start | bytes 196612
  11.6 16.7 %collective-permute-start = (f32[1,64,128]{2,1,0:T(8,128)S(1)}, f32[1,64,128]{2,1,0:T(8,128)S(1)}, u32[]{:S(2)}, u32[]{:S(2)}) collective-permute-start(f32[1,64,128]{2,1,0:T(8,128)S(1)} %get-tuple-element.93), channel_id=1, source_target_pairs={{1,0},{2,1},{3,2},{4,3},{5,4},{6,5},{7,6},{8,7},{9,8},{10,9},{11,1... | collective-permute-start | bytes 98312 | tf_op jit(solution)/shard_map/ppermute | solution.py:20
  14.2 29.7 %copy-start.6 = (f32[1,4,2,64,128]{4,1,3,2,0:T(4,128)}, f32[1,4,2,64,128]{4,1,3,2,0:T(4,128)S(1)}, u32[]{:S(2)}) copy-start(f32[1,4,2,64,128]{4,1,3,2,0:T(4,128)S(1)} %copy.36) | copy-start | bytes 786436
  14.2 29.0 %collective-permute-start.13 = (f32[4,1,64,128]{3,0,2,1:T(4,128)S(1)}, f32[4,1,64,128]{3,0,2,1:T(4,128)S(1)}, u32[]{:S(2)}, u32[]{:S(2)}) collective-permute-start(f32[4,1,64,128]{3,0,2,1:T(4,128)S(1)} %get-tuple-element.78), channel_id=1, source_target_pairs={{0,1},{1,2},{2,3},{3,4},{4,5},{5,6},{6,7},{7,8},{8,9},{9,10},{10,1... | collective-permute-start | bytes 393224 | tf_op jit(solution)/shard_map/ppermute | solution.py:17
  18.8 24.5 %collective-permute-start.12 = (f32[4,1,64,128]{3,0,2,1:T(4,128)S(1)}, f32[4,1,64,128]{3,0,2,1:T(4,128)S(1)}, u32[]{:S(2)}, u32[]{:S(2)}) collective-permute-start(f32[4,1,64,128]{3,0,2,1:T(4,128)S(1)} %get-tuple-element.79), channel_id=1, source_target_pairs={{1,0},{2,1},{3,2},{4,3},{5,4},{6,5},{7,6},{8,7},{9,8},{10,9},{11,1... | collective-permute-start | bytes 393224 | tf_op jit(solution)/shard_map/ppermute | solution.py:20
  20.3 8.4 %collective-permute-start.3 = (f32[4,1,64,128]{3,0,2,1:T(4,128)S(1)}, f32[4,1,64,128]{3,0,2,1:T(4,128)S(1)}, u32[]{:S(2)}, u32[]{:S(2)}) collective-permute-start(f32[4,1,64,128]{3,0,2,1:T(4,128)S(1)} %get-tuple-element.88), channel_id=1, source_target_pairs={{0,1},{1,2},{2,3},{3,4},{4,5},{5,6},{6,7},{7,8},{8,9},{9,10},{10,1... | collective-permute-start | bytes 393224 | tf_op jit(solution)/shard_map/ppermute | solution.py:17
  27.0 6.9 %collective-permute-start.1 = (f32[4,1,64,128]{3,0,2,1:T(4,128)S(1)}, f32[4,1,64,128]{3,0,2,1:T(4,128)S(1)}, u32[]{:S(2)}, u32[]{:S(2)}) collective-permute-start(f32[4,1,64,128]{3,0,2,1:T(4,128)S(1)} %get-tuple-element.89), channel_id=1, source_target_pairs={{1,0},{2,1},{3,2},{4,3},{5,4},{6,5},{7,6},{8,7},{9,8},{10,9},{11,1... | collective-permute-start | bytes 393224 | tf_op jit(solution)/shard_map/ppermute | solution.py:20
  28.6 15.2 %copy-start.58 = (f32[2,64,128]{2,1,0:T(8,128)}, f32[2,64,128]{2,1,0:T(8,128)S(1)}, u32[]{:S(2)}) copy-start(f32[2,64,128]{2,1,0:T(8,128)S(1)} %get-tuple-element.66) | copy-start | bytes 196612
  28.7 15.2 %copy-start.64 = (f32[2,64,128]{2,1,0:T(8,128)}, f32[2,64,128]{2,1,0:T(8,128)S(1)}, u32[]{:S(2)}) copy-start(f32[2,64,128]{2,1,0:T(8,128)S(1)} %get-tuple-element.67) | copy-start | bytes 196612
  28.7 15.2 %copy-start.70 = (f32[2,64,128]{2,1,0:T(8,128)}, f32[2,64,128]{2,1,0:T(8,128)S(1)}, u32[]{:S(2)}) copy-start(f32[2,64,128]{2,1,0:T(8,128)S(1)} %get-tuple-element.68) | copy-start | bytes 196612
  28.7 15.2 %copy-start.76 = (f32[2,64,128]{2,1,0:T(8,128)}, f32[2,64,128]{2,1,0:T(8,128)S(1)}, u32[]{:S(2)}) copy-start(f32[2,64,128]{2,1,0:T(8,128)S(1)} %get-tuple-element.69) | copy-start | bytes 196612
  28.7 15.2 %copy-start.82 = (f32[2,64,128]{2,1,0:T(8,128)}, f32[2,64,128]{2,1,0:T(8,128)S(1)}, u32[]{:S(2)}) copy-start(f32[2,64,128]{2,1,0:T(8,128)S(1)} %get-tuple-element.90) | copy-start | bytes 196612
  28.7 15.2 %copy-start.88 = (f32[2,64,128]{2,1,0:T(8,128)}, f32[2,64,128]{2,1,0:T(8,128)S(1)}, u32[]{:S(2)}) copy-start(f32[2,64,128]{2,1,0:T(8,128)S(1)} %get-tuple-element.91) | copy-start | bytes 196612
  36.9 17.5 %collective-permute-start.5 = (f32[4,1,64,128]{3,0,2,1:T(4,128)S(1)}, f32[4,1,64,128]{3,0,2,1:T(4,128)S(1)}, u32[]{:S(2)}, u32[]{:S(2)}) collective-permute-start(f32[4,1,64,128]{3,0,2,1:T(4,128)S(1)} %get-tuple-element.86), channel_id=1, source_target_pairs={{0,1},{1,2},{2,3},{3,4},{4,5},{5,6},{6,7},{7,8},{8,9},{9,10},{10,1... | collective-permute-start | bytes 393224 | tf_op jit(solution)/shard_map/ppermute | solution.py:17
  41.9 12.6 %collective-permute-start.4 = (f32[4,1,64,128]{3,0,2,1:T(4,128)S(1)}, f32[4,1,64,128]{3,0,2,1:T(4,128)S(1)}, u32[]{:S(2)}, u32[]{:S(2)}) collective-permute-start(f32[4,1,64,128]{3,0,2,1:T(4,128)S(1)} %get-tuple-element.87), channel_id=1, source_target_pairs={{1,0},{2,1},{3,2},{4,3},{5,4},{6,5},{7,6},{8,7},{9,8},{10,9},{11,1... | collective-permute-start | bytes 393224 | tf_op jit(solution)/shard_map/ppermute | solution.py:20
  43.9 10.6 %copy-start.9 = (f32[4,2,64,128]{3,0,2,1:T(4,128)S(1)}, f32[4,2,64,128]{3,0,2,1:T(4,128)}, u32[]{:S(2)}) copy-start(f32[4,2,64,128]{3,0,2,1:T(4,128)} %copy-done.8) | copy-start | bytes 786436
  45.8 23.0 %collective-permute-start.15 = (f32[4,1,64,128]{3,0,2,1:T(4,128)}, f32[4,1,64,128]{3,0,2,1:T(4,128)}, u32[]{:S(2)}, u32[]{:S(2)}) collective-permute-start(f32[4,1,64,128]{3,0,2,1:T(4,128)} %get-tuple-element.76), channel_id=1, source_target_pairs={{0,1},{1,2},{2,3},{3,4},{4,5},{5,6},{6,7},{7,8},{8,9},{9,10},{10,1... | collective-permute-start | bytes 393224 | tf_op jit(solution)/shard_map/ppermute | solution.py:17
  53.1 15.7 %collective-permute-start.14 = (f32[4,1,64,128]{3,0,2,1:T(4,128)}, f32[4,1,64,128]{3,0,2,1:T(4,128)}, u32[]{:S(2)}, u32[]{:S(2)}) collective-permute-start(f32[4,1,64,128]{3,0,2,1:T(4,128)} %get-tuple-element.77), channel_id=1, source_target_pairs={{1,0},{2,1},{3,2},{4,3},{5,4},{6,5},{7,6},{8,7},{9,8},{10,9},{11,1... | collective-permute-start | bytes 393224 | tf_op jit(solution)/shard_map/ppermute | solution.py:20
  61.5 19.1 %collective-permute-start.7 = (f32[4,1,64,128]{3,0,2,1:T(4,128)S(1)}, f32[4,1,64,128]{3,0,2,1:T(4,128)S(1)}, u32[]{:S(2)}, u32[]{:S(2)}) collective-permute-start(f32[4,1,64,128]{3,0,2,1:T(4,128)S(1)} %get-tuple-element.84), channel_id=1, source_target_pairs={{0,1},{1,2},{2,3},{3,4},{4,5},{5,6},{6,7},{7,8},{8,9},{9,10},{10,1... | collective-permute-start | bytes 393224 | tf_op jit(solution)/shard_map/ppermute | solution.py:17
  67.6 13.1 %collective-permute-start.6 = (f32[4,1,64,128]{3,0,2,1:T(4,128)S(1)}, f32[4,1,64,128]{3,0,2,1:T(4,128)S(1)}, u32[]{:S(2)}, u32[]{:S(2)}) collective-permute-start(f32[4,1,64,128]{3,0,2,1:T(4,128)S(1)} %get-tuple-element.85), channel_id=1, source_target_pairs={{1,0},{2,1},{3,2},{4,3},{5,4},{6,5},{7,6},{8,7},{9,8},{10,9},{11,1... | collective-permute-start | bytes 393224 | tf_op jit(solution)/shard_map/ppermute | solution.py:20
  74.0 19.6 %collective-permute-start.17 = (f32[4,1,64,128]{3,0,2,1:T(4,128)}, f32[4,1,64,128]{3,0,2,1:T(4,128)}, u32[]{:S(2)}, u32[]{:S(2)}) collective-permute-start(f32[4,1,64,128]{3,0,2,1:T(4,128)} %get-tuple-element.74), channel_id=1, source_target_pairs={{0,1},{1,2},{2,3},{3,4},{4,5},{5,6},{6,7},{7,8},{8,9},{9,10},{10,1... | collective-permute-start | bytes 393224 | tf_op jit(solution)/shard_map/ppermute | solution.py:17
  79.2 14.4 %collective-permute-start.16 = (f32[4,1,64,128]{3,0,2,1:T(4,128)}, f32[4,1,64,128]{3,0,2,1:T(4,128)}, u32[]{:S(2)}, u32[]{:S(2)}) collective-permute-start(f32[4,1,64,128]{3,0,2,1:T(4,128)} %get-tuple-element.75), channel_id=1, source_target_pairs={{1,0},{2,1},{3,2},{4,3},{5,4},{6,5},{7,6},{8,7},{9,8},{10,9},{11,1... | collective-permute-start | bytes 393224 | tf_op jit(solution)/shard_map/ppermute | solution.py:20
  87.7 21.4 %collective-permute-start.9 = (f32[4,1,64,128]{3,0,2,1:T(4,128)S(1)}, f32[4,1,64,128]{3,0,2,1:T(4,128)S(1)}, u32[]{:S(2)}, u32[]{:S(2)}) collective-permute-start(f32[4,1,64,128]{3,0,2,1:T(4,128)S(1)} %get-tuple-element.82), channel_id=1, source_target_pairs={{0,1},{1,2},{2,3},{3,4},{4,5},{5,6},{6,7},{7,8},{8,9},{9,10},{10,1... | collective-permute-start | bytes 393224 | tf_op jit(solution)/shard_map/ppermute | solution.py:17
  92.3 16.9 %collective-permute-start.8 = (f32[4,1,64,128]{3,0,2,1:T(4,128)S(1)}, f32[4,1,64,128]{3,0,2,1:T(4,128)S(1)}, u32[]{:S(2)}, u32[]{:S(2)}) collective-permute-start(f32[4,1,64,128]{3,0,2,1:T(4,128)S(1)} %get-tuple-element.83), channel_id=1, source_target_pairs={{1,0},{2,1},{3,2},{4,3},{5,4},{6,5},{7,6},{8,7},{9,8},{10,9},{11,1... | collective-permute-start | bytes 393224 | tf_op jit(solution)/shard_map/ppermute | solution.py:20
  95.4 11.3 %copy-start.5 = (f32[4,4,66,130]{3,0,2,1:T(4,128)S(1)}, f32[4,4,66,130]{3,0,2,1:T(4,128)}, u32[]{:S(2)}) copy-start(f32[4,4,66,130]{3,0,2,1:T(4,128)} %copy-done.4) | copy-start | bytes 1647364
  95.4 11.3 %copy-start.13 = (f32[4,2,64,128]{3,0,2,1:T(4,128)S(1)}, f32[4,2,64,128]{3,0,2,1:T(4,128)}, u32[]{:S(2)}) copy-start(f32[4,2,64,128]{3,0,2,1:T(4,128)} %scatter-add.25) | copy-start | bytes 786436
  95.4 11.3 %copy-start.51 = (f32[4,1,64,128]{3,0,2,1:T(4,128)S(1)}, f32[4,1,64,128]{3,0,2,1:T(4,128)}, u32[]{:S(2)}) copy-start(f32[4,1,64,128]{3,0,2,1:T(4,128)} %copy-done.50) | copy-start | bytes 393220
  95.4 11.3 %copy-start.55 = (f32[4,1,64,128]{3,0,2,1:T(4,128)S(1)}, f32[4,1,64,128]{3,0,2,1:T(4,128)}, u32[]{:S(2)}) copy-start(f32[4,1,64,128]{3,0,2,1:T(4,128)} %copy-done.54) | copy-start | bytes 393220
  98.4 25.1 %collective-permute-start.19 = (f32[4,1,64,128]{3,0,2,1:T(4,128)}, f32[4,1,64,128]{3,0,2,1:T(4,128)}, u32[]{:S(2)}, u32[]{:S(2)}) collective-permute-start(f32[4,1,64,128]{3,0,2,1:T(4,128)} %get-tuple-element.72), channel_id=1, source_target_pairs={{0,1},{1,2},{2,3},{3,4},{4,5},{5,6},{6,7},{7,8},{8,9},{9,10},{10,1... | collective-permute-start | bytes 393224 | tf_op jit(solution)/shard_map/ppermute | solution.py:17
  105.2 18.4 %collective-permute-start.18 = (f32[4,1,64,128]{3,0,2,1:T(4,128)}, f32[4,1,64,128]{3,0,2,1:T(4,128)}, u32[]{:S(2)}, u32[]{:S(2)}) collective-permute-start(f32[4,1,64,128]{3,0,2,1:T(4,128)} %get-tuple-element.73), channel_id=1, source_target_pairs={{1,0},{2,1},{3,2},{4,3},{5,4},{6,5},{7,6},{8,7},{9,8},{10,9},{11,1... | collective-permute-start | bytes 393224 | tf_op jit(solution)/shard_map/ppermute | solution.py:20
  115.1 10.2 %copy-start.74 = (f32[2,64,128]{2,1,0:T(8,128)S(1)}, f32[2,64,128]{2,1,0:T(8,128)}, u32[]{:S(2)}) copy-start(f32[2,64,128]{2,1,0:T(8,128)} %copy-done.70) | copy-start | bytes 196612
  115.1 10.2 %copy-start.80 = (f32[2,64,128]{2,1,0:T(8,128)S(1)}, f32[2,64,128]{2,1,0:T(8,128)}, u32[]{:S(2)}) copy-start(f32[2,64,128]{2,1,0:T(8,128)} %copy-done.76) | copy-start | bytes 196612
  116.2 23.8 %collective-permute-start.11 = (f32[4,1,64,128]{3,0,2,1:T(4,128)S(1)}, f32[4,1,64,128]{3,0,2,1:T(4,128)S(1)}, u32[]{:S(2)}, u32[]{:S(2)}) collective-permute-start(f32[4,1,64,128]{3,0,2,1:T(4,128)S(1)} %get-tuple-element.80), channel_id=1, source_target_pairs={{0,1},{1,2},{2,3},{3,4},{4,5},{5,6},{6,7},{7,8},{8,9},{9,10},{10,1... | collective-permute-start | bytes 393224 | tf_op jit(solution)/shard_map/ppermute | solution.py:17
  122.3 17.7 %collective-permute-start.10 = (f32[4,1,64,128]{3,0,2,1:T(4,128)S(1)}, f32[4,1,64,128]{3,0,2,1:T(4,128)S(1)}, u32[]{:S(2)}, u32[]{:S(2)}) collective-permute-start(f32[4,1,64,128]{3,0,2,1:T(4,128)S(1)} %get-tuple-element.81), channel_id=1, source_target_pairs={{1,0},{2,1},{3,2},{4,3},{5,4},{6,5},{7,6},{8,7},{9,8},{10,9},{11,1... | collective-permute-start | bytes 393224 | tf_op jit(solution)/shard_map/ppermute | solution.py:20
  125.3 10.8 %copy-start.1 = (f32[4,4,66,130]{3,0,2,1:T(4,128)S(1)}, f32[4,4,66,130]{3,0,2,1:T(4,128)}, u32[]{:S(2)}) copy-start(f32[4,4,66,130]{3,0,2,1:T(4,128)} %copy-done) | copy-start | bytes 1647364
  125.3 10.8 %copy-start.3 = (f32[4,4,66,130]{3,0,2,1:T(4,128)S(1)}, f32[4,4,66,130]{3,0,2,1:T(4,128)}, u32[]{:S(2)}) copy-start(f32[4,4,66,130]{3,0,2,1:T(4,128)} %copy-done.2) | copy-start | bytes 1647364
  125.3 10.8 %copy-start.16 = (f32[4,2,64,128]{3,0,2,1:T(4,128)S(1)}, f32[4,2,64,128]{3,0,2,1:T(4,128)}, u32[]{:S(2)}) copy-start(f32[4,2,64,128]{3,0,2,1:T(4,128)} %scatter-add.26) | copy-start | bytes 786436
  125.3 10.8 %copy-start.21 = (f32[4,2,64,128]{3,0,2,1:T(4,128)S(1)}, f32[4,2,64,128]{3,0,2,1:T(4,128)}, u32[]{:S(2)}) copy-start(f32[4,2,64,128]{3,0,2,1:T(4,128)} %copy-done.19) | copy-start | bytes 786436
  125.4 10.8 %copy-start.43 = (f32[4,1,64,128]{3,0,2,1:T(4,128)S(1)}, f32[4,1,64,128]{3,0,2,1:T(4,128)}, u32[]{:S(2)}) copy-start(f32[4,1,64,128]{3,0,2,1:T(4,128)} %copy-done.42) | copy-start | bytes 393220
  125.4 10.8 %copy-start.46 = (f32[4,1,64,128]{3,0,2,1:T(4,128)S(1)}, f32[4,1,64,128]{3,0,2,1:T(4,128)}, u32[]{:S(2)}) copy-start(f32[4,1,64,128]{3,0,2,1:T(4,128)} %copy-done.45) | copy-start | bytes 393220
  127.7 16.5 %copy-start.22 = (f32[4,2,64,128]{3,0,2,1:T(4,128)}, f32[4,2,64,128]{3,0,2,1:T(4,128)S(1)}, u32[]{:S(2)}) copy-start(f32[4,2,64,128]{3,0,2,1:T(4,128)S(1)} %fusion.4) | copy-start | bytes 786436
  127.7 14.3 %collective-permute-start.21 = (f32[4,1,64,128]{3,0,2,1:T(4,128)S(1)}, f32[4,1,64,128]{3,0,2,1:T(4,128)S(1)}, u32[]{:S(2)}, u32[]{:S(2)}) collective-permute-start(f32[4,1,64,128]{3,0,2,1:T(4,128)S(1)} %get-tuple-element.70), channel_id=1, source_target_pairs={{0,1},{1,2},{2,3},{3,4},{4,5},{5,6},{6,7},{7,8},{8,9},{9,10},{10,1... | collective-permute-start | bytes 393224 | tf_op jit(solution)/shard_map/ppermute | solution.py:17
  134.4 9.1 %collective-permute-start.20 = (f32[4,1,64,128]{3,0,2,1:T(4,128)S(1)}, f32[4,1,64,128]{3,0,2,1:T(4,128)S(1)}, u32[]{:S(2)}, u32[]{:S(2)}) collective-permute-start(f32[4,1,64,128]{3,0,2,1:T(4,128)S(1)} %get-tuple-element.71), channel_id=1, source_target_pairs={{1,0},{2,1},{3,2},{4,3},{5,4},{6,5},{7,6},{8,7},{9,8},{10,9},{11,1... | collective-permute-start | bytes 393224 | tf_op jit(solution)/shard_map/ppermute | solution.py:20
  (72 other events, 374.8 us)
Sparse Core Ops, SparseCore 0:
  145.9 128.7 all-reduce.12
where the time goes:
time: 472 us; the launch traced here: 471 us
  other arithmetic  135 us (29%)
  waiting for transfers between devices  129 us (27%)
  blocking collectives  75.4 us (16%)
  starting transfers between devices  75.2 us (16%)
  local copies, waits for them, and re-layouts  23 us (5%)
  between operations  17.9 us (4%)
  matrix products  15.3 us (3%)
    psum x1, waiting for transfers between devices, on_device(): summed = lax.psum(weighted, 'exp')  122 us
    scatter-add x1, other arithmetic, on_device(): jax.ops.segment_sum(summed.reshape(-1), flat_labels, num_segments=LABELS)  114 us
    psum x1, blocking collectives, on_device(): total = lax.psum(binned, 'space')  75.4 us
    ppermute x11, starting transfers between devices, extended(): lax.ppermute(lax.slice_in_dim(block, block.shape[dim] - width, None, axis...  60.2 us
    ppermute x11, starting transfers between devices, extended(): lax.ppermute(lax.slice_in_dim(block, 0, width, axis=dim), axis, backward)  15 us
    scatter-add x5, local copies, waits for them, and re-layouts, on_device(): state = state.at[0].add(pulse)  11 us
  transfers between devices with their start and end apart: 23, of which 3 were waited for; matrix products, arithmetic and copies ran while one was open for 11% of the time, Pallas kernels for 0%

commit v1 on v0

--- a/solution.py
+++ b/solution.py
@@ -101,7 +101,7 @@
         adjoint = adjoint + time_step * flow
     weighted = -0.5 * time_step * grad * permeability
     flat_labels = labels.reshape(-1)
-    summed = lax.psum(weighted, "exp")
+    summed = jnp.sum(lax.all_gather(weighted, "exp"), axis=0)
     binned = jax.ops.segment_sum(summed.reshape(-1), flat_labels, num_segments=LABELS)
     total = lax.psum(binned, "space")
     norm_factor = math.sqrt(

time: 472 us -> 411 us (0.87)
  the two profiles are of different devices: /device:TPU:8 before, /device:TPU:24 now
where the time goes in v1:
time: 411 us; the launch traced here: 409 us
  other arithmetic  137 us (33%)
  blocking collectives  75.7 us (18%)
  starting transfers between devices  75 us (18%)
  waiting for transfers between devices  65.8 us (16%)
  local copies, waits for them, and re-layouts  23 us (6%)
  between operations  17.9 us (4%)
  matrix products  15.3 us (4%)
    scatter-add x1, other arithmetic, on_device(): jax.ops.segment_sum(summed.reshape(-1), flat_labels, num_segments=LABELS)  114 us
    psum x1, blocking collectives, on_device(): total = lax.psum(binned, 'space')  75.7 us
    ppermute x11, starting transfers between devices, extended(): lax.ppermute(lax.slice_in_dim(block, block.shape[dim] - width, None, axis...  60.2 us
    all_gather x1, waiting for transfers between devices, on_device(): summed = jnp.sum(lax.all_gather(weighted, 'exp'), axis=0)  59.2 us
    ppermute x11, starting transfers between devices, extended(): lax.ppermute(lax.slice_in_dim(block, 0, width, axis=dim), axis, backward)  14.8 us
    scatter-add x5, local copies, waits for them, and re-layouts, on_device(): state = state.at[0].add(pulse)  11 us
    concatenate x11, other arithmetic, extended(): block = jnp.concatenate([low, block, high], axis=dim)  9.36 us
    dot_general x5, matrix products, on_device(): jnp.einsum('dc,dxyz->cxyz', mixing, adjoint, precision=lax.Precision.HIGH...  9.34 us
  transfers between devices with their start and end apart: 23, of which 3 were waited for; matrix products, arithmetic and copies ran while one was open for 13% of the time, Pallas kernels for 0%

profile of v1, /device:TPU:24, one launch (start us, length us, event | category | flops | bytes accessed | tf_op | source)
XLA Modules:
  0.0 409.4 jit_solution(14453021140694918377)
XLA Ops:
  8.1 3.5 collective-permute-start.2
  11.6 1.3 collective-permute-start
  12.9 1.1 copy.46
  14.1 4.6 %collective-permute-start.13 = (f32[4,1,64,128]{3,0,2,1:T(4,128)S(1)}, f32[4,1,64,128]{3,0,2,1:T(4,128)S(1)}, u32[]{:S(2)}, u32[]{:S(2)}) collective-permute-start(f32[4,1,64,128]{3,0,2,1:T(4,128)S(1)} %get-tuple-element.81), channel_id=1, source_target_pairs={{0,1},{1,2},{2,3},{3,4},{4,5},{5,6},{6,7},{7,8},{8,9},{9,10},{10,1... | collective-permute-start | bytes 393224 | tf_op jit(solution)/shard_map/ppermute | solution.py:17
  18.6 1.3 collective-permute-start.12
  20.1 4.6 %collective-permute-start.3 = (f32[4,1,64,128]{3,0,2,1:T(4,128)S(1)}, f32[4,1,64,128]{3,0,2,1:T(4,128)S(1)}, u32[]{:S(2)}, u32[]{:S(2)}) collective-permute-start(f32[4,1,64,128]{3,0,2,1:T(4,128)S(1)} %get-tuple-element.91), channel_id=1, source_target_pairs={{0,1},{1,2},{2,3},{3,4},{4,5},{5,6},{6,7},{7,8},{8,9},{9,10},{10,1... | collective-permute-start | bytes 393224 | tf_op jit(solution)/shard_map/ppermute | solution.py:17
  26.9 1.3 collective-permute-start.1
  28.6 5.2 %collective-permute-done.1 = f32[4,1,64,128]{3,0,2,1:T(4,128)S(1)} collective-permute-done((f32[4,1,64,128]{3,0,2,1:T(4,128)S(1)}, f32[4,1,64,128]{3,0,2,1:T(4,128)S(1)}, u32[]{:S(2)}, u32[]{:S(2)}) %collective-permute-start.1) | collective-permute-done | bytes 131104 | tf_op jit(solution)/shard_map/ppermute | solution.py:20
  35.4 1.3 scatter-add.24
  36.8 5.0 %collective-permute-start.5 = (f32[4,1,64,128]{3,0,2,1:T(4,128)S(1)}, f32[4,1,64,128]{3,0,2,1:T(4,128)S(1)}, u32[]{:S(2)}, u32[]{:S(2)}) collective-permute-start(f32[4,1,64,128]{3,0,2,1:T(4,128)S(1)} %get-tuple-element.89), channel_id=1, source_target_pairs={{0,1},{1,2},{2,3},{3,4},{4,5},{5,6},{6,7},{7,8},{8,9},{9,10},{10,1... | collective-permute-start | bytes 393224 | tf_op jit(solution)/shard_map/ppermute | solution.py:17
  41.7 1.3 collective-permute-start.4
  43.8 1.1 fusion.10
  45.7 7.3 %collective-permute-start.15 = (f32[4,1,64,128]{3,0,2,1:T(4,128)}, f32[4,1,64,128]{3,0,2,1:T(4,128)}, u32[]{:S(2)}, u32[]{:S(2)}) collective-permute-start(f32[4,1,64,128]{3,0,2,1:T(4,128)} %get-tuple-element.79), channel_id=1, source_target_pairs={{0,1},{1,2},{2,3},{3,4},{4,5},{5,6},{6,7},{7,8},{8,9},{9,10},{10,1... | collective-permute-start | bytes 393224 | tf_op jit(solution)/shard_map/ppermute | solution.py:17
  53.0 1.3 collective-permute-start.14
  57.5 2.8 scatter-add.25
  60.3 1.0 fusion.76
  61.4 6.0 %collective-permute-start.7 = (f32[4,1,64,128]{3,0,2,1:T(4,128)S(1)}, f32[4,1,64,128]{3,0,2,1:T(4,128)S(1)}, u32[]{:S(2)}, u32[]{:S(2)}) collective-permute-start(f32[4,1,64,128]{3,0,2,1:T(4,128)S(1)} %get-tuple-element.87), channel_id=1, source_target_pairs={{0,1},{1,2},{2,3},{3,4},{4,5},{5,6},{6,7},{7,8},{8,9},{9,10},{10,1... | collective-permute-start | bytes 393224 | tf_op jit(solution)/shard_map/ppermute | solution.py:17
  67.4 1.3 collective-permute-start.6
  68.8 1.7 select_maximum_fusion.6
  70.5 2.6 fusion.8
  73.9 5.2 %collective-permute-start.17 = (f32[4,1,64,128]{3,0,2,1:T(4,128)}, f32[4,1,64,128]{3,0,2,1:T(4,128)}, u32[]{:S(2)}, u32[]{:S(2)}) collective-permute-start(f32[4,1,64,128]{3,0,2,1:T(4,128)} %get-tuple-element.77), channel_id=1, source_target_pairs={{0,1},{1,2},{2,3},{3,4},{4,5},{5,6},{6,7},{7,8},{8,9},{9,10},{10,1... | collective-permute-start | bytes 393224 | tf_op jit(solution)/shard_map/ppermute | solution.py:17
  79.1 1.5 collective-permute-start.16
  83.7 2.8 scatter-add.26
  87.6 4.6 %collective-permute-start.9 = (f32[4,1,64,128]{3,0,2,1:T(4,128)S(1)}, f32[4,1,64,128]{3,0,2,1:T(4,128)S(1)}, u32[]{:S(2)}, u32[]{:S(2)}) collective-permute-start(f32[4,1,64,128]{3,0,2,1:T(4,128)S(1)} %get-tuple-element.85), channel_id=1, source_target_pairs={{0,1},{1,2},{2,3},{3,4},{4,5},{5,6},{6,7},{7,8},{8,9},{9,10},{10,1... | collective-permute-start | bytes 393224 | tf_op jit(solution)/shard_map/ppermute | solution.py:17
  92.2 1.3 collective-permute-start.8
  93.5 1.7 select_maximum_fusion.4
  95.3 2.3 fusion.6
  98.3 6.8 %collective-permute-start.19 = (f32[4,1,64,128]{3,0,2,1:T(4,128)}, f32[4,1,64,128]{3,0,2,1:T(4,128)}, u32[]{:S(2)}, u32[]{:S(2)}) collective-permute-start(f32[4,1,64,128]{3,0,2,1:T(4,128)} %get-tuple-element.75), channel_id=1, source_target_pairs={{0,1},{1,2},{2,3},{3,4},{4,5},{5,6},{6,7},{7,8},{8,9},{9,10},{10,1... | collective-permute-start | bytes 393224 | tf_op jit(solution)/shard_map/ppermute | solution.py:17
  105.1 1.4 collective-permute-start.18
  106.5 2.5 multiply_reduce_fusion.2
  112.2 2.8 scatter-add.29
  115.0 1.0 fusion.74
  116.1 6.0 %collective-permute-start.11 = (f32[4,1,64,128]{3,0,2,1:T(4,128)S(1)}, f32[4,1,64,128]{3,0,2,1:T(4,128)S(1)}, u32[]{:S(2)}, u32[]{:S(2)}) collective-permute-start(f32[4,1,64,128]{3,0,2,1:T(4,128)S(1)} %get-tuple-element.83), channel_id=1, source_target_pairs={{0,1},{1,2},{2,3},{3,4},{4,5},{5,6},{6,7},{7,8},{8,9},{9,10},{10,1... | collective-permute-start | bytes 393224 | tf_op jit(solution)/shard_map/ppermute | solution.py:17
  122.1 1.3 collective-permute-start.10
  123.4 1.7 select_maximum_fusion.2
  125.2 2.3 fusion.4
  127.6 6.7 %collective-permute-start.21 = (f32[4,1,64,128]{3,0,2,1:T(4,128)S(1)}, f32[4,1,64,128]{3,0,2,1:T(4,128)S(1)}, u32[]{:S(2)}, u32[]{:S(2)}) collective-permute-start(f32[4,1,64,128]{3,0,2,1:T(4,128)S(1)} %get-tuple-element.73), channel_id=1, source_target_pairs={{0,1},{1,2},{2,3},{3,4},{4,5},{5,6},{6,7},{7,8},{8,9},{9,10},{10,1... | collective-permute-start | bytes 393224 | tf_op jit(solution)/shard_map/ppermute | solution.py:17
  134.3 1.6 collective-permute-start.20
  136.0 1.9 multiply_reduce_fusion.3
  137.9 1.9 multiply_reduce_fusion.1
  141.9 1.4 collective-permute-done.20
  145.8 2.2 fusion.12
  148.2 1.3 scatter-add.36
  150.3 1.1 fusion.2
  152.1 59.2 %all-gather.3.cloned.1.call-done = f32[32,64,128]{2,1,0:T(8,128)} async-done(((f32[2,64,128]{2,1,0:T(8,128)}), f32[32,64,128]{2,1,0:T(8,128)}) %all-gather.3.cloned.1.call-update) | async-done | bytes 1048592 | tf_op jit(solution)/shard_map/all_gather | solution.py:104
  211.3 1.3 reduce_sum.69
  212.6 113.7 %scatter_custom_fusion = f32[512]{0:T(512)S(1)} fusion(s32[16384]{0:T(1024)} %bitcast.76, f32[16384]{0:T(1024)S(1)} %bitcast.75, f32[]{:T(128)} %constant.150.clone.1), kind=kCustom, calls=%fused_computation.191 | custom fusion | flops 16384 | bytes 2560 | tf_op jit(solution)/shard_map/scatter-add | solution.py:105
  326.2 75.7 %psum.7 = f32[512]{0:T(512)S(1)} all-reduce(f32[512]{0:T(512)S(1)} %scatter_custom_fusion), channel_id=1, replica_groups=mesh['exp'=16,'space'=32] {'space'}, use_global_device_ids=true, to_apply=%region_8.9 | all-reduce | flops 512 | bytes 4096 | tf_op jit(solution)/shard_map/psum | solution.py:106
  (253 shorter events, 23.1 us)
Async XLA Ops:
  7.2 12.8 %copy-start.57 = (f32[1,4,2,64,128]{4,3,2,1,0:T(8,128)S(1)}, f32[1,4,2,64,128]{4,3,2,1,0:T(8,128)}, u32[]{:S(2)}) copy-start(f32[1,4,2,64,128]{4,3,2,1,0:T(8,128)} %param.20) | copy-start | bytes 786436
  7.2 204.1 %all-gather.3.cloned.1.call-start = ((), (), s32[]{:S(2)}) async-start(), calls=%async_computation | async-start | bytes 1114112 | tf_op jit(solution)/shard_map/all_gather | solution.py:104
  8.0 16.7 %copy-start.95 = (f32[4,4]{1,0:T(4,128)S(1)}, f32[4,4]{1,0:T(4,128)}, u32[]{:S(2)}) copy-start(f32[4,4]{1,0:T(4,128)} %param.26) | copy-start | bytes 196
  8.0 16.7 %copy-start.96 = (s32[4,4]{1,0:T(4,128)S(1)}, s32[4,4]{1,0:T(4,128)}, u32[]{:S(2)}) copy-start(s32[4,4]{1,0:T(4,128)} %param.25) | copy-start | bytes 196
  8.0 20.2 %copy-start.28 = (f32[2,64,128]{2,1,0:T(8,128)S(1)}, f32[2,64,128]{2,1,0:T(8,128)}, u32[]{:S(2)}) copy-start(f32[2,64,128]{2,1,0:T(8,128)} %param.22) | copy-start | bytes 196612
  8.1 18.8 %collective-permute-start.2 = (f32[1,64,128]{2,1,0:T(8,128)S(1)}, f32[1,64,128]{2,1,0:T(8,128)S(1)}, u32[]{:S(2)}, u32[]{:S(2)}) collective-permute-start(f32[1,64,128]{2,1,0:T(8,128)S(1)} %get-tuple-element.95), channel_id=1, source_target_pairs={{0,1},{1,2},{2,3},{3,4},{4,5},{5,6},{6,7},{7,8},{8,9},{9,10},{10,1... | collective-permute-start | bytes 98312 | tf_op jit(solution)/shard_map/ppermute | solution.py:17
  11.6 16.6 %collective-permute-start = (f32[1,64,128]{2,1,0:T(8,128)S(1)}, f32[1,64,128]{2,1,0:T(8,128)S(1)}, u32[]{:S(2)}, u32[]{:S(2)}) collective-permute-start(f32[1,64,128]{2,1,0:T(8,128)S(1)} %get-tuple-element.96), channel_id=1, source_target_pairs={{1,0},{2,1},{3,2},{4,3},{5,4},{6,5},{7,6},{8,7},{9,8},{10,9},{11,1... | collective-permute-start | bytes 98312 | tf_op jit(solution)/shard_map/ppermute | solution.py:20
  14.0 29.7 %copy-start.6 = (f32[1,4,2,64,128]{4,1,3,2,0:T(4,128)}, f32[1,4,2,64,128]{4,1,3,2,0:T(4,128)S(1)}, u32[]{:S(2)}) copy-start(f32[1,4,2,64,128]{4,1,3,2,0:T(4,128)S(1)} %copy.46) | copy-start | bytes 786436
  14.1 29.0 %collective-permute-start.13 = (f32[4,1,64,128]{3,0,2,1:T(4,128)S(1)}, f32[4,1,64,128]{3,0,2,1:T(4,128)S(1)}, u32[]{:S(2)}, u32[]{:S(2)}) collective-permute-start(f32[4,1,64,128]{3,0,2,1:T(4,128)S(1)} %get-tuple-element.81), channel_id=1, source_target_pairs={{0,1},{1,2},{2,3},{3,4},{4,5},{5,6},{6,7},{7,8},{8,9},{9,10},{10,1... | collective-permute-start | bytes 393224 | tf_op jit(solution)/shard_map/ppermute | solution.py:17
  18.6 24.5 %collective-permute-start.12 = (f32[4,1,64,128]{3,0,2,1:T(4,128)S(1)}, f32[4,1,64,128]{3,0,2,1:T(4,128)S(1)}, u32[]{:S(2)}, u32[]{:S(2)}) collective-permute-start(f32[4,1,64,128]{3,0,2,1:T(4,128)S(1)} %get-tuple-element.82), channel_id=1, source_target_pairs={{1,0},{2,1},{3,2},{4,3},{5,4},{6,5},{7,6},{8,7},{9,8},{10,9},{11,1... | collective-permute-start | bytes 393224 | tf_op jit(solution)/shard_map/ppermute | solution.py:20
  20.1 8.4 %collective-permute-start.3 = (f32[4,1,64,128]{3,0,2,1:T(4,128)S(1)}, f32[4,1,64,128]{3,0,2,1:T(4,128)S(1)}, u32[]{:S(2)}, u32[]{:S(2)}) collective-permute-start(f32[4,1,64,128]{3,0,2,1:T(4,128)S(1)} %get-tuple-element.91), channel_id=1, source_target_pairs={{0,1},{1,2},{2,3},{3,4},{4,5},{5,6},{6,7},{7,8},{8,9},{9,10},{10,1... | collective-permute-start | bytes 393224 | tf_op jit(solution)/shard_map/ppermute | solution.py:17
  26.9 6.9 %collective-permute-start.1 = (f32[4,1,64,128]{3,0,2,1:T(4,128)S(1)}, f32[4,1,64,128]{3,0,2,1:T(4,128)S(1)}, u32[]{:S(2)}, u32[]{:S(2)}) collective-permute-start(f32[4,1,64,128]{3,0,2,1:T(4,128)S(1)} %get-tuple-element.92), channel_id=1, source_target_pairs={{1,0},{2,1},{3,2},{4,3},{5,4},{6,5},{7,6},{8,7},{9,8},{10,9},{11,1... | collective-permute-start | bytes 393224 | tf_op jit(solution)/shard_map/ppermute | solution.py:20
  28.5 15.2 %copy-start.58 = (f32[2,64,128]{2,1,0:T(8,128)}, f32[2,64,128]{2,1,0:T(8,128)S(1)}, u32[]{:S(2)}) copy-start(f32[2,64,128]{2,1,0:T(8,128)S(1)} %get-tuple-element.69) | copy-start | bytes 196612
  28.5 15.2 %copy-start.64 = (f32[2,64,128]{2,1,0:T(8,128)}, f32[2,64,128]{2,1,0:T(8,128)S(1)}, u32[]{:S(2)}) copy-start(f32[2,64,128]{2,1,0:T(8,128)S(1)} %get-tuple-element.70) | copy-start | bytes 196612
  28.5 15.2 %copy-start.70 = (f32[2,64,128]{2,1,0:T(8,128)}, f32[2,64,128]{2,1,0:T(8,128)S(1)}, u32[]{:S(2)}) copy-start(f32[2,64,128]{2,1,0:T(8,128)S(1)} %get-tuple-element.71) | copy-start | bytes 196612
  28.5 15.2 %copy-start.76 = (f32[2,64,128]{2,1,0:T(8,128)}, f32[2,64,128]{2,1,0:T(8,128)S(1)}, u32[]{:S(2)}) copy-start(f32[2,64,128]{2,1,0:T(8,128)S(1)} %get-tuple-element.72) | copy-start | bytes 196612
  28.6 15.2 %copy-start.82 = (f32[2,64,128]{2,1,0:T(8,128)}, f32[2,64,128]{2,1,0:T(8,128)S(1)}, u32[]{:S(2)}) copy-start(f32[2,64,128]{2,1,0:T(8,128)S(1)} %get-tuple-element.93) | copy-start | bytes 196612
  28.6 15.2 %copy-start.88 = (f32[2,64,128]{2,1,0:T(8,128)}, f32[2,64,128]{2,1,0:T(8,128)S(1)}, u32[]{:S(2)}) copy-start(f32[2,64,128]{2,1,0:T(8,128)S(1)} %get-tuple-element.94) | copy-start | bytes 196612
  36.8 17.5 %collective-permute-start.5 = (f32[4,1,64,128]{3,0,2,1:T(4,128)S(1)}, f32[4,1,64,128]{3,0,2,1:T(4,128)S(1)}, u32[]{:S(2)}, u32[]{:S(2)}) collective-permute-start(f32[4,1,64,128]{3,0,2,1:T(4,128)S(1)} %get-tuple-element.89), channel_id=1, source_target_pairs={{0,1},{1,2},{2,3},{3,4},{4,5},{5,6},{6,7},{7,8},{8,9},{9,10},{10,1... | collective-permute-start | bytes 393224 | tf_op jit(solution)/shard_map/ppermute | solution.py:17
  41.7 12.6 %collective-permute-start.4 = (f32[4,1,64,128]{3,0,2,1:T(4,128)S(1)}, f32[4,1,64,128]{3,0,2,1:T(4,128)S(1)}, u32[]{:S(2)}, u32[]{:S(2)}) collective-permute-start(f32[4,1,64,128]{3,0,2,1:T(4,128)S(1)} %get-tuple-element.90), channel_id=1, source_target_pairs={{1,0},{2,1},{3,2},{4,3},{5,4},{6,5},{7,6},{8,7},{9,8},{10,9},{11,1... | collective-permute-start | bytes 393224 | tf_op jit(solution)/shard_map/ppermute | solution.py:20
  43.8 10.6 %copy-start.9 = (f32[4,2,64,128]{3,0,2,1:T(4,128)S(1)}, f32[4,2,64,128]{3,0,2,1:T(4,128)}, u32[]{:S(2)}) copy-start(f32[4,2,64,128]{3,0,2,1:T(4,128)} %copy-done.8) | copy-start | bytes 786436
  45.7 23.0 %collective-permute-start.15 = (f32[4,1,64,128]{3,0,2,1:T(4,128)}, f32[4,1,64,128]{3,0,2,1:T(4,128)}, u32[]{:S(2)}, u32[]{:S(2)}) collective-permute-start(f32[4,1,64,128]{3,0,2,1:T(4,128)} %get-tuple-element.79), channel_id=1, source_target_pairs={{0,1},{1,2},{2,3},{3,4},{4,5},{5,6},{6,7},{7,8},{8,9},{9,10},{10,1... | collective-permute-start | bytes 393224 | tf_op jit(solution)/shard_map/ppermute | solution.py:17
  53.0 15.7 %collective-permute-start.14 = (f32[4,1,64,128]{3,0,2,1:T(4,128)}, f32[4,1,64,128]{3,0,2,1:T(4,128)}, u32[]{:S(2)}, u32[]{:S(2)}) collective-permute-start(f32[4,1,64,128]{3,0,2,1:T(4,128)} %get-tuple-element.80), channel_id=1, source_target_pairs={{1,0},{2,1},{3,2},{4,3},{5,4},{6,5},{7,6},{8,7},{9,8},{10,9},{11,1... | collective-permute-start | bytes 393224 | tf_op jit(solution)/shard_map/ppermute | solution.py:20
  61.4 19.1 %collective-permute-start.7 = (f32[4,1,64,128]{3,0,2,1:T(4,128)S(1)}, f32[4,1,64,128]{3,0,2,1:T(4,128)S(1)}, u32[]{:S(2)}, u32[]{:S(2)}) collective-permute-start(f32[4,1,64,128]{3,0,2,1:T(4,128)S(1)} %get-tuple-element.87), channel_id=1, source_target_pairs={{0,1},{1,2},{2,3},{3,4},{4,5},{5,6},{6,7},{7,8},{8,9},{9,10},{10,1... | collective-permute-start | bytes 393224 | tf_op jit(solution)/shard_map/ppermute | solution.py:17
  67.4 13.1 %collective-permute-start.6 = (f32[4,1,64,128]{3,0,2,1:T(4,128)S(1)}, f32[4,1,64,128]{3,0,2,1:T(4,128)S(1)}, u32[]{:S(2)}, u32[]{:S(2)}) collective-permute-start(f32[4,1,64,128]{3,0,2,1:T(4,128)S(1)} %get-tuple-element.88), channel_id=1, source_target_pairs={{1,0},{2,1},{3,2},{4,3},{5,4},{6,5},{7,6},{8,7},{9,8},{10,9},{11,1... | collective-permute-start | bytes 393224 | tf_op jit(solution)/shard_map/ppermute | solution.py:20
  73.9 19.6 %collective-permute-start.17 = (f32[4,1,64,128]{3,0,2,1:T(4,128)}, f32[4,1,64,128]{3,0,2,1:T(4,128)}, u32[]{:S(2)}, u32[]{:S(2)}) collective-permute-start(f32[4,1,64,128]{3,0,2,1:T(4,128)} %get-tuple-element.77), channel_id=1, source_target_pairs={{0,1},{1,2},{2,3},{3,4},{4,5},{5,6},{6,7},{7,8},{8,9},{9,10},{10,1... | collective-permute-start | bytes 393224 | tf_op jit(solution)/shard_map/ppermute | solution.py:17
  79.1 14.4 %collective-permute-start.16 = (f32[4,1,64,128]{3,0,2,1:T(4,128)}, f32[4,1,64,128]{3,0,2,1:T(4,128)}, u32[]{:S(2)}, u32[]{:S(2)}) collective-permute-start(f32[4,1,64,128]{3,0,2,1:T(4,128)} %get-tuple-element.78), channel_id=1, source_target_pairs={{1,0},{2,1},{3,2},{4,3},{5,4},{6,5},{7,6},{8,7},{9,8},{10,9},{11,1... | collective-permute-start | bytes 393224 | tf_op jit(solution)/shard_map/ppermute | solution.py:20
  87.6 21.4 %collective-permute-start.9 = (f32[4,1,64,128]{3,0,2,1:T(4,128)S(1)}, f32[4,1,64,128]{3,0,2,1:T(4,128)S(1)}, u32[]{:S(2)}, u32[]{:S(2)}) collective-permute-start(f32[4,1,64,128]{3,0,2,1:T(4,128)S(1)} %get-tuple-element.85), channel_id=1, source_target_pairs={{0,1},{1,2},{2,3},{3,4},{4,5},{5,6},{6,7},{7,8},{8,9},{9,10},{10,1... | collective-permute-start | bytes 393224 | tf_op jit(solution)/shard_map/ppermute | solution.py:17
  92.2 16.9 %collective-permute-start.8 = (f32[4,1,64,128]{3,0,2,1:T(4,128)S(1)}, f32[4,1,64,128]{3,0,2,1:T(4,128)S(1)}, u32[]{:S(2)}, u32[]{:S(2)}) collective-permute-start(f32[4,1,64,128]{3,0,2,1:T(4,128)S(1)} %get-tuple-element.86), channel_id=1, source_target_pairs={{1,0},{2,1},{3,2},{4,3},{5,4},{6,5},{7,6},{8,7},{9,8},{10,9},{11,1... | collective-permute-start | bytes 393224 | tf_op jit(solution)/shard_map/ppermute | solution.py:20
  95.2 11.3 %copy-start.5 = (f32[4,4,66,130]{3,0,2,1:T(4,128)S(1)}, f32[4,4,66,130]{3,0,2,1:T(4,128)}, u32[]{:S(2)}) copy-start(f32[4,4,66,130]{3,0,2,1:T(4,128)} %copy-done.4) | copy-start | bytes 1647364
  95.2 11.3 %copy-start.13 = (f32[4,2,64,128]{3,0,2,1:T(4,128)S(1)}, f32[4,2,64,128]{3,0,2,1:T(4,128)}, u32[]{:S(2)}) copy-start(f32[4,2,64,128]{3,0,2,1:T(4,128)} %scatter-add.25) | copy-start | bytes 786436
  95.2 11.3 %copy-start.53 = (f32[4,1,64,128]{3,0,2,1:T(4,128)S(1)}, f32[4,1,64,128]{3,0,2,1:T(4,128)}, u32[]{:S(2)}) copy-start(f32[4,1,64,128]{3,0,2,1:T(4,128)} %copy-done.52) | copy-start | bytes 393220
  95.2 11.3 %copy-start.55 = (f32[4,1,64,128]{3,0,2,1:T(4,128)S(1)}, f32[4,1,64,128]{3,0,2,1:T(4,128)}, u32[]{:S(2)}) copy-start(f32[4,1,64,128]{3,0,2,1:T(4,128)} %copy-done.54) | copy-start | bytes 393220
  98.3 25.1 %collective-permute-start.19 = (f32[4,1,64,128]{3,0,2,1:T(4,128)}, f32[4,1,64,128]{3,0,2,1:T(4,128)}, u32[]{:S(2)}, u32[]{:S(2)}) collective-permute-start(f32[4,1,64,128]{3,0,2,1:T(4,128)} %get-tuple-element.75), channel_id=1, source_target_pairs={{0,1},{1,2},{2,3},{3,4},{4,5},{5,6},{6,7},{7,8},{8,9},{9,10},{10,1... | collective-permute-start | bytes 393224 | tf_op jit(solution)/shard_map/ppermute | solution.py:17
  105.1 18.4 %collective-permute-start.18 = (f32[4,1,64,128]{3,0,2,1:T(4,128)}, f32[4,1,64,128]{3,0,2,1:T(4,128)}, u32[]{:S(2)}, u32[]{:S(2)}) collective-permute-start(f32[4,1,64,128]{3,0,2,1:T(4,128)} %get-tuple-element.76), channel_id=1, source_target_pairs={{1,0},{2,1},{3,2},{4,3},{5,4},{6,5},{7,6},{8,7},{9,8},{10,9},{11,1... | collective-permute-start | bytes 393224 | tf_op jit(solution)/shard_map/ppermute | solution.py:20
  115.0 10.2 %copy-start.74 = (f32[2,64,128]{2,1,0:T(8,128)S(1)}, f32[2,64,128]{2,1,0:T(8,128)}, u32[]{:S(2)}) copy-start(f32[2,64,128]{2,1,0:T(8,128)} %copy-done.70) | copy-start | bytes 196612
  115.0 10.2 %copy-start.80 = (f32[2,64,128]{2,1,0:T(8,128)S(1)}, f32[2,64,128]{2,1,0:T(8,128)}, u32[]{:S(2)}) copy-start(f32[2,64,128]{2,1,0:T(8,128)} %copy-done.76) | copy-start | bytes 196612
  116.1 23.8 %collective-permute-start.11 = (f32[4,1,64,128]{3,0,2,1:T(4,128)S(1)}, f32[4,1,64,128]{3,0,2,1:T(4,128)S(1)}, u32[]{:S(2)}, u32[]{:S(2)}) collective-permute-start(f32[4,1,64,128]{3,0,2,1:T(4,128)S(1)} %get-tuple-element.83), channel_id=1, source_target_pairs={{0,1},{1,2},{2,3},{3,4},{4,5},{5,6},{6,7},{7,8},{8,9},{9,10},{10,1... | collective-permute-start | bytes 393224 | tf_op jit(solution)/shard_map/ppermute | solution.py:17
  122.1 17.7 %collective-permute-start.10 = (f32[4,1,64,128]{3,0,2,1:T(4,128)S(1)}, f32[4,1,64,128]{3,0,2,1:T(4,128)S(1)}, u32[]{:S(2)}, u32[]{:S(2)}) collective-permute-start(f32[4,1,64,128]{3,0,2,1:T(4,128)S(1)} %get-tuple-element.84), channel_id=1, source_target_pairs={{1,0},{2,1},{3,2},{4,3},{5,4},{6,5},{7,6},{8,7},{9,8},{10,9},{11,1... | collective-permute-start | bytes 393224 | tf_op jit(solution)/shard_map/ppermute | solution.py:20
  125.2 10.8 %copy-start.1 = (f32[4,4,66,130]{3,0,2,1:T(4,128)S(1)}, f32[4,4,66,130]{3,0,2,1:T(4,128)}, u32[]{:S(2)}) copy-start(f32[4,4,66,130]{3,0,2,1:T(4,128)} %copy-done) | copy-start | bytes 1647364
  125.2 10.8 %copy-start.3 = (f32[4,4,66,130]{3,0,2,1:T(4,128)S(1)}, f32[4,4,66,130]{3,0,2,1:T(4,128)}, u32[]{:S(2)}) copy-start(f32[4,4,66,130]{3,0,2,1:T(4,128)} %copy-done.2) | copy-start | bytes 1647364
  125.2 10.8 %copy-start.16 = (f32[4,2,64,128]{3,0,2,1:T(4,128)S(1)}, f32[4,2,64,128]{3,0,2,1:T(4,128)}, u32[]{:S(2)}) copy-start(f32[4,2,64,128]{3,0,2,1:T(4,128)} %scatter-add.26) | copy-start | bytes 786436
  125.2 10.8 %copy-start.21 = (f32[4,2,64,128]{3,0,2,1:T(4,128)S(1)}, f32[4,2,64,128]{3,0,2,1:T(4,128)}, u32[]{:S(2)}) copy-start(f32[4,2,64,128]{3,0,2,1:T(4,128)} %copy-done.19) | copy-start | bytes 786436
  125.2 10.8 %copy-start.49 = (f32[4,1,64,128]{3,0,2,1:T(4,128)S(1)}, f32[4,1,64,128]{3,0,2,1:T(4,128)}, u32[]{:S(2)}) copy-start(f32[4,1,64,128]{3,0,2,1:T(4,128)} %copy-done.48) | copy-start | bytes 393220
  125.2 10.8 %copy-start.51 = (f32[4,1,64,128]{3,0,2,1:T(4,128)S(1)}, f32[4,1,64,128]{3,0,2,1:T(4,128)}, u32[]{:S(2)}) copy-start(f32[4,1,64,128]{3,0,2,1:T(4,128)} %copy-done.50) | copy-start | bytes 393220
  127.5 16.5 %copy-start.22 = (f32[4,2,64,128]{3,0,2,1:T(4,128)}, f32[4,2,64,128]{3,0,2,1:T(4,128)S(1)}, u32[]{:S(2)}) copy-start(f32[4,2,64,128]{3,0,2,1:T(4,128)S(1)} %fusion.4) | copy-start | bytes 786436
  127.6 14.3 %collective-permute-start.21 = (f32[4,1,64,128]{3,0,2,1:T(4,128)S(1)}, f32[4,1,64,128]{3,0,2,1:T(4,128)S(1)}, u32[]{:S(2)}, u32[]{:S(2)}) collective-permute-start(f32[4,1,64,128]{3,0,2,1:T(4,128)S(1)} %get-tuple-element.73), channel_id=1, source_target_pairs={{0,1},{1,2},{2,3},{3,4},{4,5},{5,6},{6,7},{7,8},{8,9},{9,10},{10,1... | collective-permute-start | bytes 393224 | tf_op jit(solution)/shard_map/ppermute | solution.py:17
  134.3 9.1 %collective-permute-start.20 = (f32[4,1,64,128]{3,0,2,1:T(4,128)S(1)}, f32[4,1,64,128]{3,0,2,1:T(4,128)S(1)}, u32[]{:S(2)}, u32[]{:S(2)}) collective-permute-start(f32[4,1,64,128]{3,0,2,1:T(4,128)S(1)} %get-tuple-element.74), channel_id=1, source_target_pairs={{1,0},{2,1},{3,2},{4,3},{5,4},{6,5},{7,6},{8,7},{9,8},{10,9},{11,1... | collective-permute-start | bytes 393224 | tf_op jit(solution)/shard_map/ppermute | solution.py:20
  (72 other events, 394.9 us)
Sparse Core Ops, SparseCore 0:
  145.8 65.4 all-gather.2
